TPU v7x, 32 devices: a whole 2x2x4 slice. The times are simulated.
32 devices in a mesh: user: 8 (over y, x, core), item: 4 (over z).
Axes of the slice: x: 2, y: 2, z: 4, core: 2. Of those that a mesh axis runs over, the one named last changes fastest.
Arguments:
- tokens: bfloat16 [16384, 1024], P(('user', 'item')), may hold values from -6 to 6
- lengths: int32 [32, 8], P(('user', 'item')), may hold values from 1 to 64, as said below
- destination: int32 [32, 8], P(('user', 'item')), may hold values from 0 to 7, as said below
- worker_offset: int32 [32, 8], P(('user', 'item')), may hold values from 0 to 255
- positives: int32 [16384], P(('user', 'item')), may hold values from 0 to 1023, as said below
- negatives: int32 [4, 256], replicated, may hold values from 0 to 1023, as said below
- table: bfloat16 [1024, 1024], P('item'), may hold values from -6 to 6
- in_gain: float32 [1024], replicated, may hold values from 0.1 to 1.9
- w_uvqk: bfloat16 [1024, 2048], P('item'), may hold values from -0.1875 to 0.1875
- out_gain: float32 [512], replicated, may hold values from 0.1 to 1.9
- w_out: bfloat16 [512, 1024], P(None, 'item'), may hold values from -0.25 to 0.25
Outputs:
- layer_out: bfloat16 [8192, 1024], P(('user', 'item'))
- token_grad: bfloat16 [16384, 1024], P(('user', 'item'))
- item_grad: float32 [1024, 1024], P('item', 'user')
Inputs may be any that keep to these rules, and one draw needn't show every extreme that they name: `lengths`: A device's histories lie in its rows in order from row 0 and fill at most 512 rows; every destination receives a history of exactly 64 tokens. `destination`: A device sends its 8 histories to 8 different destinations along user; the histories sent to one device by the devices of its item index, placed at their worker_offset, cover its 256 rows exactly once. `positives`: the target ids of a device lie among the 256 table rows of its item index. `negatives`: columns k * 64 to k * 64 + 63 of each group name rows held by item index k.
All inputs are finite; a program needn't handle non-finite values.
Results may differ from a plain program's by a relative error of at most 0.017.
Values may be sent and summed in bfloat16 or wider, within the bound.
A program may use at most 64 MiB of HBM per device.

v0:
```python
import jax
import jax.numpy as jnp
from jax import lax
from jax.sharding import PartitionSpec as P

HEAD = 128
TOK_DEV = 256
norm_epsilon = 1e-05
scale_epsilon = 1e-06
inverse_temp = 20.0
loss_scale = 32.0


def layer_norm(values, gain):
    center = jnp.mean(values, axis=-1, keepdims=True)
    shifted = values - center
    spread = jnp.mean(shifted * shifted, axis=-1, keepdims=True)
    return shifted * lax.rsqrt(spread + norm_epsilon) * gain


def hstu_block(rows, segment, in_gain, w_uvqk, out_gain, w_out):
    count = rows.shape[0]
    rows_f = rows.astype(jnp.float32)
    normed = layer_norm(rows_f, in_gain).astype(jnp.bfloat16)
    projected = jnp.dot(
        normed,
        lax.all_gather(w_uvqk, "item", axis=0, tiled=True),
        preferred_element_type=jnp.float32,
    )
    active = jax.nn.silu(projected).astype(jnp.bfloat16)
    width = active.shape[1] // 4
    heads = width // HEAD
    gate_u = active[:, :width]
    values_v = active[:, width : 2 * width].reshape(count, heads, HEAD)
    queries = active[:, 2 * width : 3 * width].reshape(count, heads, HEAD)
    key_rows = active[:, 3 * width :].reshape(count, heads, HEAD)
    scores = jnp.einsum(
        "qhd,khd->hqk", queries, key_rows, preferred_element_type=jnp.float32
    ) * HEAD ** (-0.5)
    order = jnp.arange(count, dtype=jnp.int32)
    allowed = (segment[:, None] == segment[None, :]) & (order[None, :] <= order[:, None])
    weights = jnp.where(allowed[None], jax.nn.silu(scores), 0.0).astype(jnp.bfloat16)
    mixed = jnp.einsum(
        "hqk,khd->qhd", weights, values_v, preferred_element_type=jnp.float32
    ).reshape(count, width)
    gated = (layer_norm(mixed, out_gain) * gate_u.astype(jnp.float32)).astype(jnp.bfloat16)
    delta = jnp.dot(
        gated, lax.all_gather(w_out, "item", axis=1, tiled=True), preferred_element_type=jnp.float32
    )
    return (rows_f + delta).astype(jnp.bfloat16)


def dispatch(rows, home_start, history_len, targets, offsets, slot_rows, user_count):
    peers = jnp.arange(user_count, dtype=jnp.int32)
    chosen = (targets[None, :] == peers[:, None]).astype(jnp.int32)
    first_row = jnp.sum(chosen * home_start[None, :], axis=1)
    sent_count = jnp.sum(chosen * history_len[None, :], axis=1)
    landing = jnp.sum(chosen * offsets[None, :], axis=1)
    within = jnp.arange(slot_rows, dtype=jnp.int32)
    picked = jnp.minimum(first_row[:, None] + within[None, :], rows.shape[0] - 1)
    filled = within[None, :] < sent_count[:, None]
    parcels = jnp.where(filled[:, :, None], rows[picked], jnp.zeros((), rows.dtype))
    labels = jnp.stack([landing, sent_count], axis=1)
    arrived, arrived_labels = (
        lax.all_to_all(parcels, "user", split_axis=0, concat_axis=0, tiled=True),
        lax.all_to_all(labels, "user", split_axis=0, concat_axis=0, tiled=True),
    )
    worker_rows = jnp.arange(TOK_DEV, dtype=jnp.int32)
    lower = arrived_labels[:, 0]
    upper = lower + arrived_labels[:, 1]
    inside = (
        (worker_rows[:, None] >= lower[None, :]) & (worker_rows[:, None] < upper[None, :])
    ).astype(jnp.int32)
    source = jnp.sum(inside * peers[None, :], axis=1)
    begin = jnp.sum(inside * lower[None, :], axis=1)
    flattened = arrived.reshape(-1, arrived.shape[-1])
    gathered = flattened[source * slot_rows + worker_rows - begin]
    return (gathered, source, arrived_labels)


def per_device(
    tokens,
    lengths,
    destination,
    worker_offset,
    positives,
    negatives,
    table,
    in_gain,
    w_uvqk,
    out_gain,
    w_out,
):
    user_count = lax.axis_size("user")
    item_count = lax.axis_size("item")
    item_here = lax.axis_index("item")
    user_here = lax.axis_index("user")
    home_rows = tokens.shape[0]
    model_width = tokens.shape[1]
    hist_count = lengths.shape[1]
    slot_rows = home_rows // hist_count
    history_len = lengths[0]
    targets = destination[0]
    offsets = worker_offset[0]
    home_start = jnp.cumsum(history_len) - history_len
    row_ids = jnp.arange(home_rows, dtype=jnp.int32)
    finished = (row_ids[:, None] >= (home_start + history_len)[None, :]).astype(jnp.int32)
    home_segment = jnp.sum(finished, axis=1)
    valid = row_ids < jnp.sum(history_len)
    home_out = hstu_block(tokens, home_segment, in_gain, w_uvqk, out_gain, w_out)
    layer_out = dispatch(
        home_out, home_start, history_len, targets, offsets, slot_rows, user_count
    )[0]
    item_rows = table.shape[0]
    table_f = table.astype(jnp.float32)
    table_scale = lax.rsqrt(jnp.mean(table_f * table_f, axis=1) + scale_epsilon)
    table_hat = table_f * table_scale[:, None]
    table_low = table_hat.astype(jnp.bfloat16)
    share = negatives.shape[1] // item_count
    owned_ids = (
        lax.dynamic_slice_in_dim(negatives, item_here * share, share, 1) - item_here * item_rows
    )
    group_rows = lax.all_to_all(
        table_low[owned_ids], "item", split_axis=0, concat_axis=0, tiled=True
    ).reshape(-1, model_width)
    positive_local = positives - item_here * item_rows
    positive_rows = table_low[positive_local]
    out_f = home_out.astype(jnp.float32)
    out_scale = lax.rsqrt(jnp.mean(out_f * out_f, axis=1) + scale_epsilon)
    out_hat = out_f * out_scale[:, None]
    out_low = out_hat.astype(jnp.bfloat16)
    factor = inverse_temp / model_width
    positive_logit = (
        jnp.einsum("rd,rd->r", out_low, positive_rows, preferred_element_type=jnp.float32) * factor
    )
    negative_logit = (
        jnp.einsum("rd,nd->rn", out_low, group_rows, preferred_element_type=jnp.float32) * factor
    )
    positive_exp = jnp.exp(positive_logit)
    negative_exp = jnp.exp(negative_logit)
    partition = positive_exp + jnp.sum(negative_exp, axis=1)
    weight = jnp.where(valid, loss_scale, 0.0)
    positive_grad = weight * (positive_exp / partition - 1.0)
    negative_grad = (weight[:, None] * negative_exp / partition[:, None]).astype(jnp.bfloat16)
    grad_hat = (
        positive_grad[:, None] * positive_rows.astype(jnp.float32)
        + jnp.dot(negative_grad, group_rows, preferred_element_type=jnp.float32)
    ) * factor
    token_grad = (
        (grad_hat - out_hat * jnp.mean(grad_hat * out_hat, axis=1, keepdims=True))
        * out_scale[:, None]
    ).astype(jnp.bfloat16)
    negative_terms = (
        jnp.einsum("rn,rd->nd", negative_grad, out_low, preferred_element_type=jnp.float32) * factor
    )
    owned_terms = lax.all_to_all(
        negative_terms.reshape(item_count, share, model_width).astype(jnp.bfloat16),
        "item",
        split_axis=0,
        concat_axis=0,
        tiled=True,
    ).astype(jnp.float32)
    positive_terms = (positive_grad * factor)[:, None] * out_low.astype(jnp.float32)
    catalog = jnp.arange(item_rows, dtype=jnp.int32)
    positive_hits = (positive_local[None, :] == catalog[:, None]).astype(jnp.float32)
    negative_hits = (owned_ids.reshape(-1)[None, :] == catalog[:, None]).astype(jnp.float32)
    row_sums = jnp.dot(positive_hits, positive_terms, precision=lax.Precision.HIGHEST)
    row_sums = row_sums + jnp.dot(
        negative_hits, owned_terms.reshape(-1, model_width), precision=lax.Precision.HIGHEST
    )
    column_width = model_width // user_count
    totals = lax.psum(row_sums.astype(jnp.bfloat16), "user").astype(jnp.float32)
    inner = jnp.mean(totals * table_hat, axis=1)
    whole = (totals - table_hat * inner[:, None]) * table_scale[:, None]
    item_grad = lax.dynamic_slice_in_dim(whole, user_here * column_width, column_width, 1)
    return (layer_out, token_grad, item_grad)


def solution(mesh):
    return jax.shard_map(
        per_device,
        mesh=mesh,
        in_specs=(
            P(("user", "item"), None),
            P(("user", "item"), None),
            P(("user", "item"), None),
            P(("user", "item"), None),
            P(("user", "item")),
            P(),
            P("item", None),
            P(),
            P("item", None),
            P(),
            P(None, "item"),
        ),
        out_specs=(P(("user", "item"), None), P(("user", "item"), None), P("item", "user")),
        check_vma=False,
    )
```

profile of v0, /device:TPU:0, one launch (start us, length us, event | category | flops | bytes accessed | tf_op | source)
XLA Modules:
  0.0 229.4 jit_solution(2644495984975450326)
XLA Ops:
  7.2 0.7 all-gather.3.cloned.1.call-update
  7.9 0.8 reduce-window.4
  8.8 1.4 fusion.62
  10.1 0.8 select_reduce_fusion.2
  11.0 0.7 copy.32
  11.7 5.2 %all-to-all-start.1 = ((s32[8,1,2]{2,1,0:T(1,128)}), s32[8,1,2]{2,1,0:T(1,128)S(1)}, u32[]{:S(2)}, u32[]{:S(2)}) async-start(s32[8,1,2]{2,1,0:T(1,128)} %copy.32), calls=%async_computation.1 | async-start | bytes 8192 | tf_op jit(solution)/shard_map/all_to_all | solution.py:66
  16.9 0.7 all-gather.5.cloned.1.call-update
  17.7 1.5 convert_reduce_fusion
  19.2 0.4 fusion.5
  19.7 0.1 convert_reduce_fusion.1
  19.8 0.2 fusion.34
  20.0 0.2 fusion.23
  20.2 0.2 fusion.58
  20.5 0.1 reshape.277
  20.6 2.0 gather_fusion.2
  22.6 2.0 gather_fusion.3
  24.6 0.7 fusion.52
  25.6 4.9 %all-to-all-start.2 = ((bf16[4,64,1024]{2,1,0:T(8,128)(2,1)}), bf16[4,64,1024]{2,1,0:T(8,128)(2,1)S(1)}, u32[]{:S(2)}, u32[]{:S(2)}) async-start(bf16[4,64,1024]{2,1,0:T(8,128)(2,1)} %bitcast.67), calls=%async_computation.2 | async-start | bytes 1048576 | tf_op jit(solution)/shard_map/all_to_all | solution.py:123
  30.5 0.1 select_reduce_fusion.1
  30.6 73.6 %all-gather.3.cloned.1.call-done = bf16[1024,2048]{1,0:T(8,128)(2,1)} async-done(((bf16[256,2048]{1,0:T(8,128)(2,1)}), bf16[1024,2048]{1,0:T(8,128)(2,1)}) %all-gather.3.cloned.1.call-update) | async-done | bytes 4194320 | tf_op jit(solution)/shard_map/all_gather | solution.py:27
  104.2 5.1 %multiply_convert_fusion = bf16[512,2048]{1,0:T(8,128)(2,1)S(1)} fusion(bf16[1024,2048]{1,0:T(8,128)(2,1)} %all-gather.3.cloned.1.call-done, bf16[512,1024]{1,0:T(8,128)(2,1)S(1)} %copy-done.1, f32[1024]{0:T(1024)S(1)} %copy-done.8, f32[512]{0:T(512)S(1)} %add_rsqrt_fusion.2, f32[512]{0:T(512)S(1)} %broadcast_multiply_fusion.3), kind=kOutput, calls=%fused_computation.5 | convolution fusion | flops 2155347968 | bytes 7348224 | tf_op jit(solution)/shard_map/dot_general | solution.py:25
  109.3 1.3 copy-done.3
  110.6 1.2 slice_bitcast_fusion.1
  111.8 1.0 copy.38
  112.8 3.4 %fusion.63 = (f32[512]{0:T(512)S(1)}, f32[4,128,512]{2,1,0:T(8,128)S(1)}) fusion(bf16[512,4,128]{0,2,1:T(8,128)(2,1)} %bitcast.72, pred[512,512]{1,0:T(8,128)(4,1)S(1)} %fusion.34, bf16[64,4,8,128]{3,2,1,0:T(8,128)(2,1)} %get-tuple-element.15, bf16[64,4,8,128]{3,2,1,0:T(8,128)(2,1)} %get-tuple-element.14), kind=kOutput, calls=%fused_computation.121 | convolution fusion | flops 544472576 | bytes 2885632 | tf_op jit(solution)/shard_map/hqk,khd->qhd/dot_general | solution.py:43
  116.2 1.3 copy.39
  117.5 0.2 fusion.29
  117.7 16.4 %all-gather.5.cloned.1.call-done = bf16[512,1024]{1,0:T(8,128)(2,1)} async-done(((bf16[512,256]{1,0:T(8,128)(2,1)}), bf16[512,1024]{1,0:T(8,128)(2,1)}) %all-gather.5.cloned.1.call-update) | async-done | bytes 1048592 | tf_op jit(solution)/shard_map/all_gather | solution.py:48
  134.1 3.0 %fusion.12 = (f32[512]{0:T(512)S(1)}, bf16[512,1024]{1,0:T(8,128)(2,1)S(1)}) fusion(bf16[512,1024]{1,0:T(8,128)(2,1)} %all-gather.5.cloned.1.call-done, f32[512,512]{1,0:T(8,128)} %copy.39, bf16[512,2048]{1,0:T(8,128)(2,1)} %copy-done.3, f32[512]{0:T(512)S(1)} %copy-done.9, f32[512]{0:T(512)S(1)} %add_rsqrt_fusion.1, f32[512]{0:T(512)S(1)} %broadcast_multiply_fusion.1, ...), kind=kOutput, calls=%fused_computation.26 | convolution fusion | flops 541588992 | bytes 4726784 | tf_op jit(solution)/shard_map/dot_general | solution.py:47
  137.1 0.5 fusion.15
  137.6 0.6 fusion.68
  138.2 0.7 broadcast_multiply_fusion
  139.0 1.3 fusion.20
  140.3 3.8 %all-to-all-start.3 = ((bf16[4,64,1024]{2,1,0:T(8,128)(2,1)}), bf16[4,64,1024]{2,1,0:T(8,128)(2,1)S(1)}, u32[]{:S(2)}, u32[]{:S(2)}) async-start(bf16[4,64,1024]{2,1,0:T(8,128)(2,1)} %bitcast.71), calls=%async_computation.3 | async-start | bytes 1048576 | tf_op jit(solution)/shard_map/all_to_all | solution.py:156
  144.2 2.8 %gather_fusion = bf16[512,1024]{1,0:T(8,128)(2,1)} fusion(bf16[512,1024]{1,0:T(8,128)(2,1)S(1)} %get-tuple-element.25, s32[1024]{0:T(1024)S(1)} %pad_clamp_fusion.3), kind=kCustom, calls=%fused_computation | custom fusion | bytes 2099200 | tf_op jit(solution)/shard_map/gather | solution.py:62
  147.0 2.4 %broadcast_select_fusion = bf16[8,64,1024]{2,1,0:T(8,128)(2,1)} fusion(bf16[8,64,1024]{2,1,0:T(8,128)(2,1)} %bitcast.65, pred[8,64]{1,0:T(8,128)(4,1)S(1)} %iota_compare_fusion.9), kind=kLoop, calls=%fused_computation.54 | loop fusion | flops 524288 | bytes 2097664 | tf_op jit(solution)/shard_map/jit(_where)/select_n | solution.py:62
  149.4 2.1 fusion.8
  151.5 5.7 %all-to-all-done.3 = bf16[4,64,1024]{2,1,0:T(8,128)(2,1)S(1)} async-done(((bf16[4,64,1024]{2,1,0:T(8,128)(2,1)}), bf16[4,64,1024]{2,1,0:T(8,128)(2,1)S(1)}, u32[]{:S(2)}, u32[]{:S(2)}) %all-to-all-start.3) | async-done | bytes 524320 | tf_op jit(solution)/shard_map/all_to_all | solution.py:156
  157.2 4.2 %all-to-all-start = ((bf16[8,64,1024]{2,1,0:T(8,128)(2,1)}), bf16[8,64,1024]{2,1,0:T(8,128)(2,1)S(1)}, u32[]{:S(2)}, u32[]{:S(2)}) async-start(bf16[8,64,1024]{2,1,0:T(8,128)(2,1)} %broadcast_select_fusion), calls=%async_computation | async-start | bytes 2097152 | tf_op jit(solution)/shard_map/all_to_all | solution.py:65
  161.5 0.3 fusion.48
  161.8 2.4 %fusion.21 = bf16[256,1024]{1,0:T(8,128)(2,1)} fusion(f32[256,1024]{1,0:T(8,128)S(1)} %fusion.48, f32[512]{0:T(512)S(1)} %get-tuple-element.8, s32[512]{0:T(512)S(1)} %get-tuple-element.13, bf16[512,1024]{1,0:T(8,128)(2,1)S(1)} %get-tuple-element.25, f32[512]{0:T(512)S(1)} %add_rsqrt_fusion), kind=kOutput, calls=%fused_computation.38 | convolution fusion | flops 1613889536 | bytes 2627584 | tf_op jit(solution)/shard_map/dot_general | solution.py:167
  164.2 3.0 %fusion.11 = bf16[512,1024]{1,0:T(8,128)(2,1)} fusion(f32[512,1024]{1,0:T(8,128)} %get-tuple-element.29, bf16[512,1024]{1,0:T(8,128)(2,1)S(1)} %get-tuple-element.25, f32[512]{0:T(512)S(1)} %broadcast_multiply_fusion.2, f32[512]{0:T(512)S(1)} %add_rsqrt_fusion), kind=kLoop, calls=%fused_computation.25 | loop fusion | flops 3145728 | bytes 4198400 | tf_op jit(solution)/shard_map/convert_element_type | solution.py:152
  167.2 11.0 %all-to-all-done = bf16[8,64,1024]{2,1,0:T(8,128)(2,1)S(1)} async-done(((bf16[8,64,1024]{2,1,0:T(8,128)(2,1)}), bf16[8,64,1024]{2,1,0:T(8,128)(2,1)S(1)}, u32[]{:S(2)}, u32[]{:S(2)}) %all-to-all-start) | async-done | bytes 1048608 | tf_op jit(solution)/shard_map/all_to_all | solution.py:65
  178.2 2.0 gather_fusion.1
  180.2 40.3 %all-reduce.2.cloned.1.call-done = bf16[256,1024]{1,0:T(8,128)(2,1)} async-done(((bf16[256,1024]{1,0:T(8,128)(2,1)}), bf16[256,1024]{1,0:T(8,128)(2,1)}) %all-reduce.2.cloned.1.call-update) | async-done | bytes 524304 | tf_op jit(solution)/shard_map/psum | solution.py:172
  220.5 1.4 multiply_reduce_fusion
  221.9 0.1 convert_element_type.84
  222.0 0.8 fusion.49
  (53 shorter events, 0.9 us)
Async XLA Ops:
  7.2 12.1 %copy-start.1 = (bf16[512,1024]{1,0:T(8,128)(2,1)S(1)}, bf16[512,1024]{1,0:T(8,128)(2,1)}, u32[]{:S(2)}) copy-start(bf16[512,1024]{1,0:T(8,128)(2,1)} %param.11) | copy-start | bytes 3145732
  7.2 12.8 %copy-start.6 = (s32[512]{0:T(512)S(1)}, s32[512]{0:T(512)}, u32[]{:S(2)}) copy-start(s32[512]{0:T(512)} %param.15) | copy-start | bytes 6148
  7.2 12.8 %copy-start = (bf16[256,1024]{1,0:T(8,128)(2,1)S(1)}, bf16[256,1024]{1,0:T(8,128)(2,1)}, u32[]{:S(2)}) copy-start(bf16[256,1024]{1,0:T(8,128)(2,1)} %param.17) | copy-start | bytes 1572868
  7.2 97.0 %all-gather.3.cloned.1.call-start = ((), (), s32[]{:S(2)}) async-start(), calls=%async_computation.4 | async-start | bytes 5242880 | tf_op jit(solution)/shard_map/all_gather | solution.py:27
  11.7 13.9 %all-to-all-start.1 = ((s32[8,1,2]{2,1,0:T(1,128)}), s32[8,1,2]{2,1,0:T(1,128)S(1)}, u32[]{:S(2)}, u32[]{:S(2)}) async-start(s32[8,1,2]{2,1,0:T(1,128)} %copy.32), calls=%async_computation.1 | async-start | bytes 8192 | tf_op jit(solution)/shard_map/all_to_all | solution.py:66
  16.9 3.5 %copy-start.7 = (s32[4,256]{1,0:T(4,128)S(1)}, s32[4,256]{1,0:T(4,128)}, u32[]{:S(2)}) copy-start(s32[4,256]{1,0:T(4,128)} %param.16) | copy-start | bytes 12292
  16.9 117.2 %all-gather.5.cloned.1.call-start = ((), (), s32[]{:S(2)}) async-start(), calls=%async_computation.5 | async-start | bytes 1310720 | tf_op jit(solution)/shard_map/all_gather | solution.py:48
  22.6 81.6 %copy-start.8 = (f32[1024]{0:T(1024)S(1)}, f32[1024]{0:T(1024)}, u32[]{:S(2)}) copy-start(f32[1024]{0:T(1024)} %param.18) | copy-start | bytes 12292
  25.6 112.0 %all-to-all-start.2 = ((bf16[4,64,1024]{2,1,0:T(8,128)(2,1)}), bf16[4,64,1024]{2,1,0:T(8,128)(2,1)S(1)}, u32[]{:S(2)}, u32[]{:S(2)}) async-start(bf16[4,64,1024]{2,1,0:T(8,128)(2,1)} %bitcast.67), calls=%async_computation.2 | async-start | bytes 1048576 | tf_op jit(solution)/shard_map/all_to_all | solution.py:123
  109.3 1.4 copy-start.3
  116.2 17.9 %copy-start.9 = (f32[512]{0:T(512)S(1)}, f32[512]{0:T(512)}, u32[]{:S(2)}) copy-start(f32[512]{0:T(512)} %param.20) | copy-start | bytes 6148
  137.6 2.7 %copy-start.4 = (bf16[4,64,1024]{2,1,0:T(8,128)(2,1)}, bf16[4,64,1024]{2,1,0:T(8,128)(2,1)S(1)}, u32[]{:S(2)}) copy-start(bf16[4,64,1024]{2,1,0:T(8,128)(2,1)S(1)} %all-to-all-done.2) | copy-start | bytes 1572868
  138.2 0.8 copy-start.10
  140.3 16.9 %all-to-all-start.3 = ((bf16[4,64,1024]{2,1,0:T(8,128)(2,1)}), bf16[4,64,1024]{2,1,0:T(8,128)(2,1)S(1)}, u32[]{:S(2)}, u32[]{:S(2)}) async-start(bf16[4,64,1024]{2,1,0:T(8,128)(2,1)} %bitcast.71), calls=%async_computation.3 | async-start | bytes 1048576 | tf_op jit(solution)/shard_map/all_to_all | solution.py:156
  147.0 2.4 %copy-start.5 = (bf16[4,64,1024]{2,1,0:T(8,128)(2,1)S(1)}, bf16[4,64,1024]{2,1,0:T(8,128)(2,1)}, u32[]{:S(2)}) copy-start(bf16[4,64,1024]{2,1,0:T(8,128)(2,1)} %copy-done.4) | copy-start | bytes 1572868
  147.0 2.4 %copy-start.11 = (f32[512,256]{0,1:T(8,128)S(1)}, f32[512,256]{0,1:T(8,128)}, u32[]{:S(2)}) copy-start(f32[512,256]{0,1:T(8,128)} %copy-done.10) | copy-start | bytes 1572868
  157.2 21.0 %all-to-all-start = ((bf16[8,64,1024]{2,1,0:T(8,128)(2,1)}), bf16[8,64,1024]{2,1,0:T(8,128)(2,1)S(1)}, u32[]{:S(2)}, u32[]{:S(2)}) async-start(bf16[8,64,1024]{2,1,0:T(8,128)(2,1)} %broadcast_select_fusion), calls=%async_computation | async-start | bytes 2097152 | tf_op jit(solution)/shard_map/all_to_all | solution.py:65
  161.5 59.0 %all-reduce.2.cloned.1.call-start = ((), (), s32[]{:S(2)}) async-start(), calls=%async_computation.6 | async-start | bytes 1048576 | tf_op jit(solution)/shard_map/psum | solution.py:172
  220.5 1.4 copy-start.2
Sparse Core Ops, SparseCore 0:
  9.6 94.5 all-gather.2
  105.7 28.3 all-gather.4
  165.4 55.0 all-reduce.1
where the time goes:
time: 230 us; the launch traced here: 229 us
  waiting for transfers between devices  148 us (64%)
  starting transfers between devices  18.2 us (8%)
  matrix products  18.1 us (8%)
  other arithmetic  15.9 us (7%)
  local copies, waits for them, and re-layouts  14.7 us (6%)
  between operations  14 us (6%)
    all_gather x1, waiting for transfers between devices, hstu_block(): lax.all_gather(w_uvqk, 'item', axis=0, tiled=True)  73.6 us
    psum x1, waiting for transfers between devices, per_device(): totals = lax.psum(row_sums.astype(jnp.bfloat16), 'user').astype(jnp.float32)  40.3 us
    all_gather x1, waiting for transfers between devices, hstu_block(): lax.all_gather(w_out, 'item', axis=1, tiled=True)  16.4 us
    all_to_all x1, waiting for transfers between devices, dispatch(): lax.all_to_all(parcels, 'user', split_axis=0, concat_axis=0, tiled=True)  11 us
    all_to_all x1, waiting for transfers between devices, per_device(): lax.all_to_all(negative_terms.reshape(item_count, share, model_width).ast...  5.72 us
    all_to_all x1, starting transfers between devices, dispatch(): lax.all_to_all(labels, 'user', split_axis=0, concat_axis=0, tiled=True)  5.2 us
    dot_general x1, matrix products, hstu_block(): jnp.dot(normed, lax.all_gather(w_uvqk, 'item', axis=0, tiled=True), prefe...  5.07 us
    all_to_all x1, starting transfers between devices, per_device(): lax.all_to_all(table_low[owned_ids], 'item', split_axis=0, concat_axis=0,...  4.85 us
  transfers between devices with their start and end apart: 7, of which 5 were waited for; matrix products, arithmetic and copies ran while one was open for 18% of the time, Pallas kernels for 0%

commit v1 on v0

--- a/solution.py
+++ b/solution.py
@@ -22,11 +22,14 @@
     count = rows.shape[0]
     rows_f = rows.astype(jnp.float32)
     normed = layer_norm(rows_f, in_gain).astype(jnp.bfloat16)
-    projected = jnp.dot(
-        normed,
-        lax.all_gather(w_uvqk, "item", axis=0, tiled=True),
-        preferred_element_type=jnp.float32,
-    )
+
+    def change_values(inp):
+        far_arr = jnp.concatenate(
+            lax.all_to_all(jnp.stack([inp] * lax.axis_size("item"), 0), "item", 0, 0), 0
+        )
+        return far_arr
+
+    projected = jnp.dot(normed, change_values(w_uvqk), preferred_element_type=jnp.float32)
     active = jax.nn.silu(projected).astype(jnp.bfloat16)
     width = active.shape[1] // 4
     heads = width // HEAD

time: 230 us -> 253 us (1.10)
  waiting for transfers between devices: 148 us -> 161 us
  blocking collectives: 0 us -> 9.68 us
  local copies, waits for them, and re-layouts: 14.7 us -> 17.9 us
    all_to_all x1, waiting for transfers between devices: 0.01 us -> 103 us  [change_values(): lax.all_to_all(jnp.stack([inp] * lax.axis_size('item'), 0), 'item', 0, 0)]
    all_gather x1 -> x0, waiting for transfers between devices: 73.6 us -> none  [hstu_block(): lax.all_gather(w_uvqk, 'item', axis=0, tiled=True)]
    all_gather x1, waiting for transfers between devices: 16.4 us -> 0.01 us  [hstu_block(): lax.all_gather(w_out, 'item', axis=1, tiled=True)]
    all_to_all x0 -> x1, blocking collectives: none -> 9.68 us  [dispatch(): lax.all_to_all(labels, 'user', split_axis=0, concat_axis=0, tiled=True)]
    another operation x0 -> x1, local copies, waits for them, and re-layouts: none -> 3.73 us  [change_values(): jnp.stack([inp] * lax.axis_size('item'), 0)]
  transfers between devices with their start and end apart: 7 -> 6, of which waited for: 5 -> 4; matrix products, arithmetic and copies ran while one was open for 18% -> 15% of each run, Pallas kernels for 0% -> 0%
where the time goes in v1:
time: 253 us; the launch traced here: 252 us
  waiting for transfers between devices  161 us (64%)
  matrix products  18.1 us (7%)
  local copies, waits for them, and re-layouts  17.9 us (7%)
  starting transfers between devices  17.2 us (7%)
  other arithmetic  14.4 us (6%)
  between operations  14.3 us (6%)
  blocking collectives  9.68 us (4%)
    all_to_all x1, waiting for transfers between devices, change_values(): lax.all_to_all(jnp.stack([inp] * lax.axis_size('item'), 0), 'item', 0, 0)  103 us
    psum x1, waiting for transfers between devices, per_device(): totals = lax.psum(row_sums.astype(jnp.bfloat16), 'user').astype(jnp.float32)  40.3 us
    all_to_all x1, waiting for transfers between devices, dispatch(): lax.all_to_all(parcels, 'user', split_axis=0, concat_axis=0, tiled=True)  10.9 us
    all_to_all x1, blocking collectives, dispatch(): lax.all_to_all(labels, 'user', split_axis=0, concat_axis=0, tiled=True)  9.68 us
    all_to_all x1, waiting for transfers between devices, per_device(): lax.all_to_all(negative_terms.reshape(item_count, share, model_width).ast...  6.06 us
    all_to_all x1, starting transfers between devices, per_device(): lax.all_to_all(negative_terms.reshape(item_count, share, model_width).ast...  5.1 us
  transfers between devices with their start and end apart: 6, of which 4 were waited for; matrix products, arithmetic and copies ran while one was open for 15% of the time, Pallas kernels for 0%

profile of v1, /device:TPU:0, one launch (start us, length us, event | category | flops | bytes accessed | tf_op | source)
XLA Modules:
  0.0 252.4 jit_solution(4557234465850791253)
XLA Ops:
  7.2 0.8 reduce-window.4
  8.0 1.3 fusion.62
  9.3 0.8 select_reduce_fusion.2
  10.2 9.7 %all_to_all.32 = s32[8,1,2]{2,1,0:T(1,128)S(1)} all-to-all(s32[8,1,2]{2,1,0:T(1,128)S(1)} %copy.32), channel_id=1, replica_groups=mesh['user'=8,'item'=4] {'user'}, dimensions={0} | all-to-all | bytes 128 | tf_op jit(solution)/shard_map/all_to_all | solution.py:69
  19.9 3.7 %stack.6 = bf16[4,256,2048]{2,1,0:T(8,128)(2,1)} broadcast(bf16[256,2048]{1,0:T(8,128)(2,1)} %param.19), dimensions={1,2} | broadcast | bytes 5242880 | tf_op jit(solution)/shard_map/stack | solution.py:28
  23.6 5.0 %all-to-all-start = ((bf16[4,256,2048]{2,1,0:T(8,128)(2,1)}), bf16[4,256,2048]{2,1,0:T(8,128)(2,1)}, u32[]{:S(2)}, u32[]{:S(2)}) async-start(bf16[4,256,2048]{2,1,0:T(8,128)(2,1)} %stack.6), calls=%async_computation | async-start | bytes 8388608 | tf_op jit(solution)/shard_map/all_to_all | solution.py:28
  28.7 0.7 all-gather.2.cloned.1.call-update
  29.5 0.1 reshape.283
  29.6 0.2 fusion.23
  29.8 0.2 fusion.58
  29.9 2.1 gather_fusion.2
  32.0 2.0 gather_fusion.3
  34.2 0.6 fusion.52
  34.9 0.1 convert_reduce_fusion.1
  35.0 0.2 convert_reduce_fusion
  35.2 0.4 fusion.5
  35.7 0.2 fusion.34
  36.0 0.1 select_reduce_fusion.1
  36.1 102.8 %all-to-all-done = bf16[4,256,2048]{2,1,0:T(8,128)(2,1)} async-done(((bf16[4,256,2048]{2,1,0:T(8,128)(2,1)}), bf16[4,256,2048]{2,1,0:T(8,128)(2,1)}, u32[]{:S(2)}, u32[]{:S(2)}) %all-to-all-start) | async-done | bytes 4194336 | tf_op jit(solution)/shard_map/all_to_all | solution.py:28
  138.9 3.5 %all-to-all-start.3 = ((bf16[4,64,1024]{2,1,0:T(8,128)(2,1)}), bf16[4,64,1024]{2,1,0:T(8,128)(2,1)S(1)}, u32[]{:S(2)}, u32[]{:S(2)}) async-start(bf16[4,64,1024]{2,1,0:T(8,128)(2,1)} %bitcast.22), calls=%async_computation.3 | async-start | bytes 1048576 | tf_op jit(solution)/shard_map/all_to_all | solution.py:126
  142.4 5.1 %multiply_convert_fusion = bf16[512,2048]{1,0:T(8,128)(2,1)S(1)} fusion(bf16[1024,2048]{1,0:T(8,128)(2,1)} %bitcast.2, bf16[512,1024]{1,0:T(8,128)(2,1)S(1)} %copy-done.1, f32[1024]{0:T(1024)S(1)} %copy-done.8, f32[512]{0:T(512)S(1)} %add_rsqrt_fusion.2, f32[512]{0:T(512)S(1)} %broadcast_multiply_fusion.3), kind=kOutput, calls=%fused_computation.5 | convolution fusion | flops 2155347968 | bytes 7348224 | tf_op jit(solution)/shard_map/dot_general | solution.py:32
  147.5 1.3 copy-done.3
  148.8 1.2 slice_bitcast_fusion.1
  150.0 1.0 copy.38
  151.0 3.4 %fusion.63 = (f32[512]{0:T(512)S(1)}, f32[4,128,512]{2,1,0:T(8,128)S(1)}) fusion(bf16[512,4,128]{0,2,1:T(8,128)(2,1)} %bitcast.72, pred[512,512]{1,0:T(8,128)(4,1)S(1)} %fusion.34, bf16[64,4,8,128]{3,2,1,0:T(8,128)(2,1)} %get-tuple-element.15, bf16[64,4,8,128]{3,2,1,0:T(8,128)(2,1)} %get-tuple-element.14), kind=kOutput, calls=%fused_computation.121 | convolution fusion | flops 544472576 | bytes 2885632 | tf_op jit(solution)/shard_map/hqk,khd->qhd/dot_general | solution.py:46
  154.5 1.3 copy.39
  155.8 0.2 fusion.29
  156.0 3.0 %fusion.12 = (f32[512]{0:T(512)S(1)}, bf16[512,1024]{1,0:T(8,128)(2,1)S(1)}) fusion(bf16[512,1024]{1,0:T(8,128)(2,1)} %all-gather.2.cloned.1.call-done, f32[512,512]{1,0:T(8,128)} %copy.39, bf16[512,2048]{1,0:T(8,128)(2,1)} %copy-done.3, f32[512]{0:T(512)S(1)} %copy-done.9, f32[512]{0:T(512)S(1)} %add_rsqrt_fusion.1, f32[512]{0:T(512)S(1)} %broadcast_multiply_fusion.1, ...), kind=kOutput, calls=%fused_computation.26 | convolution fusion | flops 541588992 | bytes 4726784 | tf_op jit(solution)/shard_map/dot_general | solution.py:50
  158.9 0.5 fusion.15
  159.5 0.6 fusion.68
  160.1 0.7 broadcast_multiply_fusion
  160.8 0.1 copy-done.10
  160.9 1.3 fusion.20
  162.2 5.1 %all-to-all-start.4 = ((bf16[4,64,1024]{2,1,0:T(8,128)(2,1)}), bf16[4,64,1024]{2,1,0:T(8,128)(2,1)S(1)}, u32[]{:S(2)}, u32[]{:S(2)}) async-start(bf16[4,64,1024]{2,1,0:T(8,128)(2,1)} %bitcast.71), calls=%async_computation.4 | async-start | bytes 1048576 | tf_op jit(solution)/shard_map/all_to_all | solution.py:159
  167.3 2.8 %gather_fusion = bf16[512,1024]{1,0:T(8,128)(2,1)} fusion(bf16[512,1024]{1,0:T(8,128)(2,1)S(1)} %get-tuple-element.25, s32[1024]{0:T(1024)S(1)} %pad_clamp_fusion.3), kind=kCustom, calls=%fused_computation | custom fusion | bytes 2099200 | tf_op jit(solution)/shard_map/gather | solution.py:65
  170.1 2.4 broadcast_select_fusion
  172.6 2.1 fusion.8
  174.6 6.1 %all-to-all-done.4 = bf16[4,64,1024]{2,1,0:T(8,128)(2,1)S(1)} async-done(((bf16[4,64,1024]{2,1,0:T(8,128)(2,1)}), bf16[4,64,1024]{2,1,0:T(8,128)(2,1)S(1)}, u32[]{:S(2)}, u32[]{:S(2)}) %all-to-all-start.4) | async-done | bytes 524320 | tf_op jit(solution)/shard_map/all_to_all | solution.py:159
  180.7 3.6 %all-to-all-start.1 = ((bf16[8,64,1024]{2,1,0:T(8,128)(2,1)}), bf16[8,64,1024]{2,1,0:T(8,128)(2,1)S(1)}, u32[]{:S(2)}, u32[]{:S(2)}) async-start(bf16[8,64,1024]{2,1,0:T(8,128)(2,1)} %broadcast_select_fusion), calls=%async_computation.1 | async-start | bytes 2097152 | tf_op jit(solution)/shard_map/all_to_all | solution.py:68
  184.3 0.3 fusion.48
  184.6 2.4 fusion.21
  187.1 3.0 %fusion.11 = bf16[512,1024]{1,0:T(8,128)(2,1)} fusion(f32[512,1024]{1,0:T(8,128)} %get-tuple-element.29, bf16[512,1024]{1,0:T(8,128)(2,1)S(1)} %get-tuple-element.25, f32[512]{0:T(512)S(1)} %broadcast_multiply_fusion.2, f32[512]{0:T(512)S(1)} %add_rsqrt_fusion), kind=kLoop, calls=%fused_computation.25 | loop fusion | flops 3145728 | bytes 4198400 | tf_op jit(solution)/shard_map/convert_element_type | solution.py:155
  190.1 10.9 %all-to-all-done.1 = bf16[8,64,1024]{2,1,0:T(8,128)(2,1)S(1)} async-done(((bf16[8,64,1024]{2,1,0:T(8,128)(2,1)}), bf16[8,64,1024]{2,1,0:T(8,128)(2,1)S(1)}, u32[]{:S(2)}, u32[]{:S(2)}) %all-to-all-start.1) | async-done | bytes 1048608 | tf_op jit(solution)/shard_map/all_to_all | solution.py:68
  201.0 2.0 gather_fusion.1
  203.0 40.3 %all-reduce.2.cloned.1.call-done = bf16[256,1024]{1,0:T(8,128)(2,1)} async-done(((bf16[256,1024]{1,0:T(8,128)(2,1)}), bf16[256,1024]{1,0:T(8,128)(2,1)}) %all-reduce.2.cloned.1.call-update) | async-done | bytes 524304 | tf_op jit(solution)/shard_map/psum | solution.py:175
  243.2 1.4 multiply_reduce_fusion
  244.7 0.1 convert_element_type.84
  244.8 0.8 fusion.49
  (52 shorter events, 0.8 us)
Async XLA Ops:
  23.6 5.7 %copy-start.7 = (s32[4,256]{1,0:T(4,128)S(1)}, s32[4,256]{1,0:T(4,128)}, u32[]{:S(2)}) copy-start(s32[4,256]{1,0:T(4,128)} %param.16) | copy-start | bytes 12292
  23.6 5.9 %copy-start.6 = (s32[512]{0:T(512)S(1)}, s32[512]{0:T(512)}, u32[]{:S(2)}) copy-start(s32[512]{0:T(512)} %param.15) | copy-start | bytes 6148
  23.6 5.9 %copy-start = (bf16[256,1024]{1,0:T(8,128)(2,1)S(1)}, bf16[256,1024]{1,0:T(8,128)(2,1)}, u32[]{:S(2)}) copy-start(bf16[256,1024]{1,0:T(8,128)(2,1)} %param.17) | copy-start | bytes 1572868
  23.6 115.3 %all-to-all-start = ((bf16[4,256,2048]{2,1,0:T(8,128)(2,1)}), bf16[4,256,2048]{2,1,0:T(8,128)(2,1)}, u32[]{:S(2)}, u32[]{:S(2)}) async-start(bf16[4,256,2048]{2,1,0:T(8,128)(2,1)} %stack.6), calls=%async_computation | async-start | bytes 8388608 | tf_op jit(solution)/shard_map/all_to_all | solution.py:28
  28.6 127.3 %all-gather.2.cloned.1.call-start = ((), (), s32[]{:S(2)}) async-start(), calls=%async_computation.5 | async-start | bytes 1310720 | tf_op jit(solution)/shard_map/all_gather | solution.py:51
  32.0 3.0 %copy-start.1 = (bf16[512,1024]{1,0:T(8,128)(2,1)S(1)}, bf16[512,1024]{1,0:T(8,128)(2,1)}, u32[]{:S(2)}) copy-start(bf16[512,1024]{1,0:T(8,128)(2,1)} %param.11) | copy-start | bytes 3145732
  34.0 108.4 %copy-start.8 = (f32[1024]{0:T(1024)S(1)}, f32[1024]{0:T(1024)}, u32[]{:S(2)}) copy-start(f32[1024]{0:T(1024)} %param.18) | copy-start | bytes 12292
  138.9 20.5 %all-to-all-start.3 = ((bf16[4,64,1024]{2,1,0:T(8,128)(2,1)}), bf16[4,64,1024]{2,1,0:T(8,128)(2,1)S(1)}, u32[]{:S(2)}, u32[]{:S(2)}) async-start(bf16[4,64,1024]{2,1,0:T(8,128)(2,1)} %bitcast.22), calls=%async_computation.3 | async-start | bytes 1048576 | tf_op jit(solution)/shard_map/all_to_all | solution.py:126
  147.5 1.4 copy-start.3
  154.4 1.5 copy-start.9
  159.5 2.7 %copy-start.4 = (bf16[4,64,1024]{2,1,0:T(8,128)(2,1)}, bf16[4,64,1024]{2,1,0:T(8,128)(2,1)S(1)}, u32[]{:S(2)}) copy-start(bf16[4,64,1024]{2,1,0:T(8,128)(2,1)S(1)} %all-to-all-done.3) | copy-start | bytes 1572868
  160.1 0.8 copy-start.10
  162.2 18.5 %all-to-all-start.4 = ((bf16[4,64,1024]{2,1,0:T(8,128)(2,1)}), bf16[4,64,1024]{2,1,0:T(8,128)(2,1)S(1)}, u32[]{:S(2)}, u32[]{:S(2)}) async-start(bf16[4,64,1024]{2,1,0:T(8,128)(2,1)} %bitcast.71), calls=%async_computation.4 | async-start | bytes 1048576 | tf_op jit(solution)/shard_map/all_to_all | solution.py:159
  170.1 2.4 copy-start.5
  170.1 2.4 copy-start.11
  180.7 20.3 %all-to-all-start.1 = ((bf16[8,64,1024]{2,1,0:T(8,128)(2,1)}), bf16[8,64,1024]{2,1,0:T(8,128)(2,1)S(1)}, u32[]{:S(2)}, u32[]{:S(2)}) async-start(bf16[8,64,1024]{2,1,0:T(8,128)(2,1)} %broadcast_select_fusion), calls=%async_computation.1 | async-start | bytes 2097152 | tf_op jit(solution)/shard_map/all_to_all | solution.py:68
  184.3 59.0 %all-reduce.2.cloned.1.call-start = ((), (), s32[]{:S(2)}) async-start(), calls=%async_computation.6 | async-start | bytes 1048576 | tf_op jit(solution)/shard_map/psum | solution.py:175
  243.2 1.4 copy-start.2
Sparse Core Ops, SparseCore 0:
  31.0 53.3 all-gather.1
  188.2 55.0 all-reduce.1
